TPU v7x, 512 devices: a whole 4x4x16 slice. The times are simulated.
512 devices in a mesh: tile: 32 (over z, core), chan: 16 (over y, x).
Axes of the slice: x: 4, y: 4, z: 16, core: 2. Of those that a mesh axis runs over, the one named last changes fastest.
Arguments:
- fields: float32 [64, 1024, 411], P('chan', 'tile'), may hold values from -12 to 12
- diffusivity: float32 [64, 1024], P('chan', 'tile'), may hold values from 0.02 to 0.24
- owners: int32 [4096, 1], replicated, may hold values from 0 to 31; in each aligned block of 128 rows (0 to 127, 128 to 255, ...) at most 8 rows name the same one
- observed: bfloat16 [8192, 6144], P('tile', 'chan'), may hold values from -6 to 6
- usable: int32 [8192], P('tile'), may hold values 0 or 1
- w_hidden: bfloat16 [411, 2048], P(None, 'chan'), may hold values from -0.3125 to 0.3125
- b_hidden: float32 [2048], P('chan'), may hold values from -3 to 3
- w_radiance: bfloat16 [2048, 6144], P(None, 'chan'), may hold values from -0.125 to 0.125
- b_radiance: float32 [6144], P('chan'), may hold values from -3 to 3
- inv_cov: bfloat16 [6144, 6144], P('tile', 'chan'), may hold values from -6 to 22
Outputs:
- gradient: float32 [64, 1024, 411], P('chan', 'tile')
Inputs may be any that keep to these rules, and one draw needn't show every extreme that they name: `owners`: in each tile's block of 128 consecutive entries no owner appears more than 8 times, and in some blocks one appears exactly 8 times.
All inputs are finite; a program needn't handle non-finite values. No bound on the sum of `usable` on one device may be relied on, other than what follows from the above.
Results may differ from a plain program's by a relative error of at most 0.0045.
Values may be sent and summed in bfloat16 or wider, within the bound.
A program may use at most 64 MiB of HBM per device.

v0:
```python
import jax
import jax.numpy as jnp
from jax import lax
from jax.sharding import PartitionSpec as P


def padded_2(value, sides, width, wrap):
    for axis, dim in sides:
        devices, length = (lax.axis_size(axis), value.shape[dim])
        up = [(i, (i + 1) % devices) for i in range(devices if wrap else devices - 1)]
        down = [(j, i) for i, j in up]
        last = lax.slice_in_dim(value, length - width, length, axis=dim)
        first = lax.slice_in_dim(value, 0, width, axis=dim)
        before = lax.ppermute(last, axis, up)
        after = lax.ppermute(first, axis, down)
        value = jnp.concatenate([before, value, after], axis=dim)
    return value


def add_rims(values):
    rowwise = padded_2(values, (("chan", 0),), 1, False)
    return padded_2(rowwise, (("tile", 1),), 1, True)


def body(
    fields,
    diffusivity,
    owners,
    observed,
    usable,
    w_hidden,
    b_hidden,
    w_radiance,
    b_radiance,
    inv_cov,
):
    tile_count = lax.axis_size("tile")
    chan_count = lax.axis_size("chan")
    tile_index = lax.axis_index("tile")
    chan_index = lax.axis_index("chan")
    slot_count = observed.shape[0]
    capacity = slot_count // tile_count
    cells_across, cells_along, features = fields.shape
    own_cols = cells_across // 4 * (cells_along // 4)
    tile_cols = chan_count * own_cols
    hidden_dev = w_hidden.shape[1]
    owner_table = owners[:, 0].reshape(tile_count, tile_cols)
    owner_hits = (
        owner_table[:, :, None] == jnp.arange(tile_count, dtype=jnp.int32)[None, None, :]
    ).astype(jnp.int32)
    before = jnp.sum((jnp.cumsum(owner_hits, axis=1) - owner_hits) * owner_hits, axis=2)
    tallies = jnp.sum(owner_hits, axis=1)
    slot_of = lax.dynamic_index_in_dim(
        owner_table * capacity + before, tile_index, 0, keepdims=False
    )
    arriving = lax.dynamic_index_in_dim(tallies, tile_index, 1, keepdims=False)
    occupied = (jnp.arange(capacity, dtype=jnp.int32)[None, :] < arriving[:, None]).reshape(
        slot_count
    )
    grouped = fields.reshape(cells_across // 4, 4, cells_along // 4, 4, features)
    columns = (
        (jnp.sum(grouped, axis=(1, 3)) * 0.0625).reshape(own_cols, features).astype(jnp.bfloat16)
    )
    placer = (slot_of[None, :] == jnp.arange(slot_count, dtype=jnp.int32)[:, None]).astype(
        jnp.bfloat16
    )
    picks = placer
    outgoing = jnp.dot(
        picks,
        lax.all_gather(columns, "chan", axis=0, tiled=True),
        preferred_element_type=jnp.float32,
    )
    incoming = lax.all_to_all(
        outgoing.astype(jnp.bfloat16), "tile", split_axis=0, concat_axis=0, tiled=True
    )
    preact = lax.dot_general(
        w_hidden, incoming, (((0,), (1,)), ((), ())), preferred_element_type=jnp.float32
    )
    preact = preact + b_hidden[:, None]
    squash = jax.nn.sigmoid(preact)
    active = (preact * squash).astype(jnp.bfloat16)
    weights = w_radiance
    radiance = lax.dot_general(
        lax.all_gather(active, "chan", axis=0, tiled=True),
        weights,
        (((0,), (0,)), ((), ())),
        preferred_element_type=jnp.float32,
    )
    radiance = radiance + b_radiance[None, :]
    in_use = usable.astype(jnp.float32) * occupied.astype(jnp.float32)
    departure = ((radiance - observed.astype(jnp.float32)) * in_use[:, None]).astype(jnp.bfloat16)
    all_depart = lax.all_gather(departure, "chan", axis=1, tiled=True)
    picks = all_depart
    cotangent = jnp.dot(
        picks,
        lax.all_gather(inv_cov, "tile", axis=0, tiled=True),
        preferred_element_type=jnp.float32,
    )
    cotangent = cotangent.astype(jnp.bfloat16)
    weights = w_radiance
    full_sum = lax.psum(
        lax.dot_general(
            weights, cotangent, (((1,), (1,)), ((), ())), preferred_element_type=jnp.float32
        ),
        "chan",
    )
    grad_hidden = lax.dynamic_slice_in_dim(full_sum, chan_index * hidden_dev, hidden_dev, 0)
    slope_term = squash * (1.0 + preact * (1.0 - squash))
    grad_pre = (grad_hidden * slope_term).astype(jnp.bfloat16)
    part_grad = lax.dot_general(
        grad_pre, w_hidden, (((0,), (1,)), ((), ())), preferred_element_type=jnp.float32
    )
    summed_grad = lax.psum(part_grad, "chan")
    returned = lax.all_to_all(summed_grad, "tile", split_axis=0, concat_axis=0, tiled=True)
    own_slots = lax.dynamic_slice_in_dim(slot_of, chan_index * own_cols, own_cols, 0)
    column_grad = jnp.take(returned, own_slots, axis=0)
    spread = jnp.repeat(
        column_grad.reshape(cells_across // 4, cells_along // 4, features), 4, axis=0
    )
    adjoint = jnp.repeat(spread, 4, axis=1) * 0.0625
    kappa_root = jnp.sqrt(diffusivity)
    root_rim = add_rims(kappa_root)
    coef_north = (kappa_root * root_rim[2:, 1:-1])[:, :, None]
    coef_south = (kappa_root * root_rim[:-2, 1:-1])[:, :, None]
    coef_east = (kappa_root * root_rim[1:-1, 2:])[:, :, None]
    coef_west = (kappa_root * root_rim[1:-1, :-2])[:, :, None]
    for sweep_index in range(2):
        padded = add_rims(adjoint)
        adjoint = (
            adjoint
            + coef_north * (padded[2:, 1:-1] - adjoint)
            + coef_south * (padded[:-2, 1:-1] - adjoint)
            + coef_east * (padded[1:-1, 2:] - adjoint)
            + coef_west * (padded[1:-1, :-2] - adjoint)
        )
    return adjoint


def solution(mesh):
    placed = (
        P("chan", "tile", None),
        P("chan", "tile"),
        P(),
        P("tile", "chan"),
        P("tile"),
        P(None, "chan"),
        P("chan"),
        P(None, "chan"),
        P("chan"),
        P("tile", "chan"),
    )
    return jax.shard_map(
        body, mesh=mesh, in_specs=placed, out_specs=P("chan", "tile", None), check_vma=False
    )
```

profile of v0, /device:TPU:6, one launch (start us, length us, event | category | flops | bytes accessed | tf_op | source)
XLA Modules:
  0.0 599.1 jit_solution(5220718163068988109)
XLA Ops:
  6.6 0.0 all-gather.4.cloned.1.call-start
  6.6 0.9 copy.26
  7.5 1.0 reduce_sum.35
  8.6 3.3 convert_reduce_fusion
  12.0 26.5 %all_gather.12 = bf16[128,411]{1,0:T(8,128)(2,1)S(1)} all-gather(bf16[8,411]{1,0:T(8,128)(2,1)S(1)} %multiply_convert_fusion.3), channel_id=1, replica_groups=mesh['tile'=32,'chan'=16] {'chan'}, dimensions={0}, use_global_device_ids=true | all-gather | bytes 111792 | tf_op jit(solution)/shard_map/all_gather | solution.py:70
  38.5 0.2 dynamic-slice_reduce_fusion
  38.6 0.3 convolution_convert_fusion
  38.9 0.1 copy.29
  39.1 35.1 %all_to_all.24 = bf16[32,8,411]{2,1,0:T(8,128)(2,1)S(1)} all-to-all(bf16[32,8,411]{2,1,0:T(8,128)(2,1)S(1)} %bitcast.26), channel_id=1, replica_groups=mesh['tile'=32,'chan'=16] {'tile'}, dimensions={0} | all-to-all | bytes 420864 | tf_op jit(solution)/shard_map/all_to_all | solution.py:73
  74.2 0.9 multiply_convert_fusion.1
  75.1 0.0 all-gather.4.cloned.1.call-update
  75.1 0.0 all-gather.6.cloned.1.call-start
  75.2 0.2 dynamic-slice_reduce_fusion.1
  75.3 0.1 iota_compare_fusion.4
  75.4 0.1 lt.53
  75.5 47.4 %all-gather.4.cloned.1.call-done = bf16[2048,256]{0,1:T(8,128)(2,1)} async-done(((bf16[128,256]{0,1:T(8,128)(2,1)}), bf16[2048,256]{0,1:T(8,128)(2,1)}) %all-gather.4.cloned.1.call-update) | async-done | bytes 1048592 | tf_op jit(solution)/shard_map/all_gather | solution.py:84
  122.9 2.6 fusion.6
  125.5 0.0 all-gather.6.cloned.1.call-update
  125.6 0.0 all-gather.8.cloned.1.call-start
  125.6 0.7 all-gather.8.cloned.1.call-update
  126.3 0.0 all-reduce.3.cloned.1.call-start
  126.3 66.2 %all-gather.6.cloned.1.call-done = bf16[256,6144]{1,0:T(8,128)(2,1)} async-done(((bf16[256,384]{1,0:T(8,128)(2,1)}), bf16[256,6144]{1,0:T(8,128)(2,1)}) %all-gather.6.cloned.1.call-update) | async-done | bytes 3145744 | tf_op jit(solution)/shard_map/all_gather | solution.py:92
  192.5 75.9 %all-gather.8.cloned.1.call-done = bf16[6144,384]{1,0:T(8,128)(2,1)} async-done(((bf16[192,384]{1,0:T(8,128)(2,1)}), bf16[6144,384]{1,0:T(8,128)(2,1)}) %all-gather.8.cloned.1.call-update) | async-done | bytes 4718608 | tf_op jit(solution)/shard_map/all_gather | solution.py:96
  268.4 7.1 %convolution_bitcast_fusion = f32[2048,256]{0,1:T(8,128)} fusion(bf16[2048,384]{1,0:T(8,128)(2,1)S(1)} %copy-done, bf16[256,6144]{1,0:T(8,128)(2,1)} %all-gather.6.cloned.1.call-done, bf16[6144,384]{1,0:T(8,128)(2,1)} %all-gather.8.cloned.1.call-done), kind=kOutput, calls=%fused_computation.5 | convolution fusion | flops 1610711040 | bytes 11534336 | tf_op jit(solution)/shard_map/dot_general | solution.py:102
  275.5 0.0 all-reduce.3.cloned.1.call-update
  275.5 0.0 all-reduce.5.cloned.1.call-start
  275.6 118.8 %all-reduce.3.cloned.1.call-done = f32[2048,256]{0,1:T(8,128)} async-done(((f32[2048,256]{0,1:T(8,128)}), f32[2048,256]{0,1:T(8,128)}) %all-reduce.3.cloned.1.call-update) | async-done | bytes 2097168 | tf_op jit(solution)/shard_map/psum | solution.py:101
  394.4 2.0 convolution_bitcast_fusion.1
  396.3 0.0 all-reduce.5.cloned.1.call-update
  396.3 117.1 %all-reduce.5.cloned.1.call-done = f32[32,8,411]{2,1,0:T(8,128)} async-done(((f32[32,8,411]{2,1,0:T(8,128)}), f32[32,8,411]{2,1,0:T(8,128)}) %all-reduce.5.cloned.1.call-update) | async-done | bytes 420880 | tf_op jit(solution)/shard_map/psum | solution.py:113
  513.4 12.6 %all-to-all-start.1 = ((f32[32,8,411]{2,1,0:T(8,128)}), f32[32,8,411]{2,1,0:T(8,128)S(1)}, u32[]{:S(2)}, u32[]{:S(2)}) async-start(f32[32,8,411]{2,1,0:T(8,128)} %all-reduce.5.cloned.1.call-done), calls=%async_computation.1 | async-start | bytes 1048576 | tf_op jit(solution)/shard_map/all_to_all | solution.py:114
  526.1 3.4 collective-permute-start.2
  529.4 2.5 collective-permute-start
  531.9 0.2 dynamic-slice_reduce_fusion.2
  532.1 0.0 collective-permute-done.2
  532.2 4.8 collective-permute-done
  537.0 0.1 fusion.40
  537.1 1.7 collective-permute-start.4
  538.8 0.0 collective-permute-start.6
  538.8 21.3 %all-to-all-done.1 = f32[32,8,411]{2,1,0:T(8,128)S(1)} async-done(((f32[32,8,411]{2,1,0:T(8,128)}), f32[32,8,411]{2,1,0:T(8,128)S(1)}, u32[]{:S(2)}, u32[]{:S(2)}) %all-to-all-start.1) | async-done | bytes 420896 | tf_op jit(solution)/shard_map/all_to_all | solution.py:114
  560.0 0.6 gather_fusion
  560.6 0.1 select_multiply_fusion
  560.7 3.4 collective-permute-start.3
  564.1 2.5 collective-permute-start.1
  566.6 0.0 collective-permute-done.4
  566.6 0.0 collective-permute-done.6
  566.6 0.1 pad_maximum_fusion.25
  566.7 0.2 collective-permute-done.3
  566.9 5.5 collective-permute-done.1
  572.4 0.0 collective-permute-start.5
  572.5 0.5 collective-permute-start.7
  573.0 0.1 slice_multiply_fusion.3
  573.0 0.8 collective-permute-done.5
  573.9 2.9 collective-permute-done.7
  576.8 0.2 fusion.23
  577.0 1.9 collective-permute-start.9
  579.0 3.9 collective-permute-start.8
  582.9 0.3 collective-permute-done.9
  583.2 4.0 collective-permute-done.8
  587.3 0.0 collective-permute-start.10
  587.3 0.5 collective-permute-start.11
  587.8 0.9 collective-permute-done.10
  588.7 2.9 collective-permute-done.11
  591.6 0.9 fusion.11
  (33 shorter events, 0.3 us)
Async XLA Ops:
  6.5 116.4 %copy-start = (bf16[2048,384]{1,0:T(8,128)(2,1)S(1)}, bf16[2048,384]{1,0:T(8,128)(2,1)}, u32[]{:S(2)}) copy-start(bf16[2048,384]{1,0:T(8,128)(2,1)} %param.17) | copy-start | bytes 4718596
  6.5 67.7 %copy-start.1 = (bf16[411,128]{1,0:T(8,128)(2,1)S(1)}, bf16[411,128]{1,0:T(8,128)(2,1)}, u32[]{:S(2)}) copy-start(bf16[411,128]{1,0:T(8,128)(2,1)} %param.15) | copy-start | bytes 315652
  6.5 67.7 %copy-start.6 = (f32[128]{0:T(128)S(1)}, f32[128]{0:T(128)}, u32[]{:S(2)}) copy-start(f32[128]{0:T(128)} %param.16) | copy-start | bytes 1540
  6.5 69.0 %copy-start.3 = (s32[256]{0:T(256)S(1)}, s32[256]{0:T(256)}, u32[]{:S(2)}) copy-start(s32[256]{0:T(256)} %param.14) | copy-start | bytes 3076
  6.5 116.4 %copy-start.5 = (f32[384]{0:T(512)S(1)}, f32[384]{0:T(512)}, u32[]{:S(2)}) copy-start(f32[384]{0:T(512)} %param.18) | copy-start | bytes 4612
  6.5 116.4 %copy-start.4 = (bf16[256,384]{1,0:T(8,128)(2,1)S(1)}, bf16[256,384]{1,0:T(8,128)(2,1)}, u32[]{:S(2)}) copy-start(bf16[256,384]{1,0:T(8,128)(2,1)} %param.13) | copy-start | bytes 589828
  6.6 116.4 %all-gather.4.cloned.1.call-start = ((), (), s32[]{:S(2)}) async-start(), calls=%async_computation.2 | async-start | bytes 1114112 | tf_op jit(solution)/shard_map/all_gather | solution.py:84
  75.1 117.4 %all-gather.6.cloned.1.call-start = ((), (), s32[]{:S(2)}) async-start(), calls=%async_computation.3 | async-start | bytes 3342336 | tf_op jit(solution)/shard_map/all_gather | solution.py:92
  125.6 142.8 %all-gather.8.cloned.1.call-start = ((), (), s32[]{:S(2)}) async-start(), calls=%async_computation.4 | async-start | bytes 4866048 | tf_op jit(solution)/shard_map/all_gather | solution.py:96
  126.3 268.1 %all-reduce.3.cloned.1.call-start = ((), (), s32[]{:S(2)}) async-start(), calls=%async_computation.5 | async-start | bytes 4194304 | tf_op jit(solution)/shard_map/psum | solution.py:101
  275.5 250.5 %copy-start.2 = (f32[4,32]{1,0:T(4,128)S(1)}, f32[4,32]{1,0:T(4,128)}, u32[]{:S(2)}) copy-start(f32[4,32]{1,0:T(4,128)} %param.11) | copy-start | bytes 1540
  275.5 237.9 %all-reduce.5.cloned.1.call-start = ((), (), s32[]{:S(2)}) async-start(), calls=%async_computation.6 | async-start | bytes 1048576 | tf_op jit(solution)/shard_map/psum | solution.py:113
  513.4 46.6 %all-to-all-start.1 = ((f32[32,8,411]{2,1,0:T(8,128)}), f32[32,8,411]{2,1,0:T(8,128)S(1)}, u32[]{:S(2)}, u32[]{:S(2)}) async-start(f32[32,8,411]{2,1,0:T(8,128)} %all-reduce.5.cloned.1.call-done), calls=%async_computation.1 | async-start | bytes 1048576 | tf_op jit(solution)/shard_map/all_to_all | solution.py:114
  526.1 6.1 %collective-permute-start.2 = (f32[1,32]{1,0:T(1,128)S(1)}, f32[1,32]{1,0:T(1,128)S(1)}, u32[]{:S(2)}, u32[]{:S(2)}) collective-permute-start(f32[1,32]{1,0:T(1,128)S(1)} %get-tuple-element.23), channel_id=1, source_target_pairs={{0,1},{1,2},{2,3},{3,4},{4,5},{5,6},{6,7},{7,8},{8,9},{9,10},{10,1... | collective-permute-start | bytes 392 | tf_op jit(solution)/shard_map/ppermute | solution.py:14
  529.4 7.6 %collective-permute-start = (f32[1,32]{1,0:T(1,128)S(1)}, f32[1,32]{1,0:T(1,128)S(1)}, u32[]{:S(2)}, u32[]{:S(2)}) collective-permute-start(f32[1,32]{1,0:T(1,128)S(1)} %get-tuple-element.24), channel_id=1, source_target_pairs={{1,0},{2,1},{3,2},{4,3},{5,4},{6,5},{7,6},{8,7},{9,8},{10,9},{11,1... | collective-permute-start | bytes 392 | tf_op jit(solution)/shard_map/ppermute | solution.py:15
  537.1 29.5 %collective-permute-start.4 = (f32[6,1]{1,0:T(8,128)S(1)}, f32[6,1]{1,0:T(8,128)S(1)}, u32[]{:S(2)}, u32[]{:S(2)}) collective-permute-start(f32[6,1]{1,0:T(8,128)S(1)} %get-tuple-element.13), channel_id=1, source_target_pairs={{16,0},{32,16},{48,32},{64,48},{80,64},{96,80},{112,96},{128,112},... | collective-permute-start | bytes 80 | tf_op jit(solution)/shard_map/ppermute | solution.py:15
  538.8 27.8 %collective-permute-start.6 = (f32[6,1]{1,0:T(8,128)S(1)}, f32[6,1]{1,0:T(8,128)S(1)}, u32[]{:S(2)}, u32[]{:S(2)}) collective-permute-start(f32[6,1]{1,0:T(8,128)S(1)} %get-tuple-element.14), channel_id=1, source_target_pairs={{0,16},{16,32},{32,48},{48,64},{64,80},{80,96},{96,112},{112,128},... | collective-permute-start | bytes 80 | tf_op jit(solution)/shard_map/ppermute | solution.py:14
  560.7 6.2 %collective-permute-start.3 = (f32[1,32,411]{2,1,0:T(8,128)S(1)}, f32[1,32,411]{2,1,0:T(8,128)S(1)}, u32[]{:S(2)}, u32[]{:S(2)}) collective-permute-start(f32[1,32,411]{2,1,0:T(8,128)S(1)} %mul.151), channel_id=1, source_target_pairs={{0,1},{1,2},{2,3},{3,4},{4,5},{5,6},{6,7},{7,8},{8,9},{9,10},{10,1... | collective-permute-start | bytes 157832 | tf_op jit(solution)/shard_map/ppermute | solution.py:14
  564.1 8.3 %collective-permute-start.1 = (f32[1,32,411]{2,1,0:T(8,128)S(1)}, f32[1,32,411]{2,1,0:T(8,128)S(1)}, u32[]{:S(2)}, u32[]{:S(2)}) collective-permute-start(f32[1,32,411]{2,1,0:T(8,128)S(1)} %mul.151), channel_id=1, source_target_pairs={{1,0},{2,1},{3,2},{4,3},{5,4},{6,5},{7,6},{8,7},{9,8},{10,9},{11,1... | collective-permute-start | bytes 157832 | tf_op jit(solution)/shard_map/ppermute | solution.py:15
  572.4 1.4 collective-permute-start.5
  572.5 4.3 collective-permute-start.7
  577.0 6.2 %collective-permute-start.9 = (f32[1,32,411]{2,1,0:T(8,128)S(1)}, f32[1,32,411]{2,1,0:T(8,128)S(1)}, u32[]{:S(2)}, u32[]{:S(2)}) collective-permute-start(f32[1,32,411]{2,1,0:T(8,128)S(1)} %get-tuple-element.11), channel_id=1, source_target_pairs={{0,1},{1,2},{2,3},{3,4},{4,5},{5,6},{6,7},{7,8},{8,9},{9,10},{10,1... | collective-permute-start | bytes 157832 | tf_op jit(solution)/shard_map/ppermute | solution.py:14
  579.0 8.3 %collective-permute-start.8 = (f32[1,32,411]{2,1,0:T(8,128)S(1)}, f32[1,32,411]{2,1,0:T(8,128)S(1)}, u32[]{:S(2)}, u32[]{:S(2)}) collective-permute-start(f32[1,32,411]{2,1,0:T(8,128)S(1)} %get-tuple-element.12), channel_id=1, source_target_pairs={{1,0},{2,1},{3,2},{4,3},{5,4},{6,5},{7,6},{8,7},{9,8},{10,9},{11,1... | collective-permute-start | bytes 157832 | tf_op jit(solution)/shard_map/ppermute | solution.py:15
  587.3 1.4 collective-permute-start.10
  587.3 4.3 collective-permute-start.11
Sparse Core Ops, SparseCore 0:
  75.2 47.6 all-gather.3
  125.9 66.5 all-gather.5
  194.7 73.6 all-gather.7
  275.7 118.6 all-reduce.2
  397.4 115.9 all-reduce.4
where the time goes:
time: 600 us; the launch traced here: 599 us
  waiting for transfers between devices  470 us (78%)
  blocking collectives  61.6 us (10%)
  starting transfers between devices  33 us (6%)
  between operations  13.5 us (2%)
  matrix products  12.8 us (2%)
    psum x1, waiting for transfers between devices, body(): lax.psum(lax.dot_general(weights, cotangent, (((1,), (1,)), ((), ())), pr...  119 us
    psum x1, waiting for transfers between devices, body(): summed_grad = lax.psum(part_grad, 'chan')  117 us
    all_gather x1, waiting for transfers between devices, body(): lax.all_gather(inv_cov, 'tile', axis=0, tiled=True)  75.9 us
    all_gather x1, waiting for transfers between devices, body(): all_depart = lax.all_gather(departure, 'chan', axis=1, tiled=True)  66.2 us
    all_gather x1, waiting for transfers between devices, body(): lax.all_gather(active, 'chan', axis=0, tiled=True)  47.4 us
    all_to_all x1, blocking collectives, body(): lax.all_to_all(outgoing.astype(jnp.bfloat16), 'tile', split_axis=0, conca...  35.1 us
    all_gather x1, blocking collectives, body(): lax.all_gather(columns, 'chan', axis=0, tiled=True)  26.5 us
    all_to_all x1, waiting for transfers between devices, body(): lax.all_to_all(summed_grad, 'tile', split_axis=0, concat_axis=0, tiled=True)  21.3 us
  transfers between devices with their start and end apart: 18, of which 15 were waited for; matrix products, arithmetic and copies ran while one was open for 0% of the time, Pallas kernels for 0%

commit v1 on v0

--- a/solution.py
+++ b/solution.py
@@ -110,7 +110,7 @@
     part_grad = lax.dot_general(
         grad_pre, w_hidden, (((0,), (1,)), ((), ())), preferred_element_type=jnp.float32
     )
-    summed_grad = lax.psum(part_grad, "chan")
+    summed_grad = jnp.sum(lax.all_gather(part_grad, "chan"), axis=0)
     returned = lax.all_to_all(summed_grad, "tile", split_axis=0, concat_axis=0, tiled=True)
     own_slots = lax.dynamic_slice_in_dim(slot_of, chan_index * own_cols, own_cols, 0)
     column_grad = jnp.take(returned, own_slots, axis=0)

time: 600 us -> 576 us (0.960)
  waiting for transfers between devices: 470 us -> 438 us
  local copies, waits for them, and re-layouts: 2.51 us -> 9.52 us
    psum x1 -> x0, waiting for transfers between devices: 117 us -> none  [body(): summed_grad = lax.psum(part_grad, 'chan')]
    all_gather x0 -> x1, waiting for transfers between devices: none -> 85.3 us  [body(): summed_grad = jnp.sum(lax.all_gather(part_grad, 'chan'), axis=0)]
    unnamed x14 -> x15, local copies, waits for them, and re-layouts: 0.03 us -> 6.04 us
where the time goes in v1:
time: 576 us
  waiting for transfers between devices  438 us (76%)
  blocking collectives  61.6 us (11%)
  starting transfers between devices  33.2 us (6%)
  between operations  13.5 us (2%)
  matrix products  12.8 us (2%)
  local copies, waits for them, and re-layouts  9.52 us (2%)
  other arithmetic  7.14 us (1%)
    psum x1, waiting for transfers between devices, body(): lax.psum(lax.dot_general(weights, cotangent, (((1,), (1,)), ((), ())), pr...  119 us
    all_gather x1, waiting for transfers between devices, body(): summed_grad = jnp.sum(lax.all_gather(part_grad, 'chan'), axis=0)  85.3 us
    all_gather x1, waiting for transfers between devices, body(): lax.all_gather(inv_cov, 'tile', axis=0, tiled=True)  75.9 us
    all_gather x1, waiting for transfers between devices, body(): all_depart = lax.all_gather(departure, 'chan', axis=1, tiled=True)  66.2 us
    all_gather x1, waiting for transfers between devices, body(): lax.all_gather(active, 'chan', axis=0, tiled=True)  47.4 us
    all_to_all x1, blocking collectives, body(): lax.all_to_all(outgoing.astype(jnp.bfloat16), 'tile', split_axis=0, conca...  35.1 us
    all_gather x1, blocking collectives, body(): lax.all_gather(columns, 'chan', axis=0, tiled=True)  26.5 us
    all_to_all x1, waiting for transfers between devices, body(): lax.all_to_all(summed_grad, 'tile', split_axis=0, concat_axis=0, tiled=True)  21.3 us
  transfers between devices with their start and end apart: 18, of which 15 were waited for; matrix products, arithmetic and copies ran while one was open for 0% of the time, Pallas kernels for 0%

profile of v1, /device:TPU:6, one launch (start us, length us, event | category | flops | bytes accessed | tf_op | source)
XLA Modules:
  0.0 575.6 jit_solution(11115896413589544427)
XLA Ops:
  6.6 0.0 all-gather.6.cloned.1.call-start
  6.6 0.9 copy.24
  7.5 1.0 reduce_sum.44
  8.6 3.3 convert_reduce_fusion
  12.0 26.5 %all_gather.18 = bf16[128,411]{1,0:T(8,128)(2,1)S(1)} all-gather(bf16[8,411]{1,0:T(8,128)(2,1)S(1)} %multiply_convert_fusion.3), channel_id=1, replica_groups=mesh['tile'=32,'chan'=16] {'chan'}, dimensions={0}, use_global_device_ids=true | all-gather | bytes 111792 | tf_op jit(solution)/shard_map/all_gather | solution.py:70
  38.5 0.2 dynamic-slice_reduce_fusion
  38.6 0.3 convolution_convert_fusion
  38.9 0.1 copy.27
  39.1 35.1 %all_to_all.24 = bf16[32,8,411]{2,1,0:T(8,128)(2,1)S(1)} all-to-all(bf16[32,8,411]{2,1,0:T(8,128)(2,1)S(1)} %bitcast.33), channel_id=1, replica_groups=mesh['tile'=32,'chan'=16] {'tile'}, dimensions={0} | all-to-all | bytes 420864 | tf_op jit(solution)/shard_map/all_to_all | solution.py:73
  74.2 0.9 multiply_convert_fusion.1
  75.1 0.0 all-gather.6.cloned.1.call-update
  75.1 0.0 all-gather.8.cloned.1.call-start
  75.1 0.2 dynamic-slice_reduce_fusion.1
  75.3 0.1 iota_compare_fusion.4
  75.4 0.1 lt.53
  75.5 47.4 %all-gather.6.cloned.1.call-done = bf16[2048,256]{0,1:T(8,128)(2,1)} async-done(((bf16[128,256]{0,1:T(8,128)(2,1)}), bf16[2048,256]{0,1:T(8,128)(2,1)}) %all-gather.6.cloned.1.call-update) | async-done | bytes 1048592 | tf_op jit(solution)/shard_map/all_gather | solution.py:84
  122.9 2.6 fusion.6
  125.5 0.0 all-gather.8.cloned.1.call-update
  125.6 0.0 all-gather.10.cloned.1.call-start
  125.6 0.7 all-gather.10.cloned.1.call-update
  126.3 0.0 all-reduce.2.cloned.1.call-start
  126.3 66.2 %all-gather.8.cloned.1.call-done = bf16[256,6144]{1,0:T(8,128)(2,1)} async-done(((bf16[256,384]{1,0:T(8,128)(2,1)}), bf16[256,6144]{1,0:T(8,128)(2,1)}) %all-gather.8.cloned.1.call-update) | async-done | bytes 3145744 | tf_op jit(solution)/shard_map/all_gather | solution.py:92
  192.5 75.9 %all-gather.10.cloned.1.call-done = bf16[6144,384]{1,0:T(8,128)(2,1)} async-done(((bf16[192,384]{1,0:T(8,128)(2,1)}), bf16[6144,384]{1,0:T(8,128)(2,1)}) %all-gather.10.cloned.1.call-update) | async-done | bytes 4718608 | tf_op jit(solution)/shard_map/all_gather | solution.py:96
  268.4 7.1 %convolution_bitcast_fusion = f32[2048,256]{0,1:T(8,128)} fusion(bf16[2048,384]{1,0:T(8,128)(2,1)S(1)} %copy-done, bf16[256,6144]{1,0:T(8,128)(2,1)} %all-gather.8.cloned.1.call-done, bf16[6144,384]{1,0:T(8,128)(2,1)} %all-gather.10.cloned.1.call-done), kind=kOutput, calls=%fused_computation.6 | convolution fusion | flops 1610711040 | bytes 11534336 | tf_op jit(solution)/shard_map/dot_general | solution.py:102
  275.5 0.0 all-reduce.2.cloned.1.call-update
  275.5 0.2 all-gather.12.cloned.1.call-start
  275.8 118.6 %all-reduce.2.cloned.1.call-done = f32[2048,256]{0,1:T(8,128)} async-done(((f32[2048,256]{0,1:T(8,128)}), f32[2048,256]{0,1:T(8,128)}) %all-reduce.2.cloned.1.call-update) | async-done | bytes 2097168 | tf_op jit(solution)/shard_map/psum | solution.py:101
  394.4 1.9 fusion.34
  396.3 0.0 all-gather.12.cloned.1.call-update
  396.3 85.3 %all-gather.12.cloned.1.call-done = f32[4096,411]{0,1:T(8,128)} async-done(((f32[256,411]{0,1:T(8,128)}), f32[4096,411]{0,1:T(8,128)}) %all-gather.12.cloned.1.call-update) | async-done | bytes 6733840 | tf_op jit(solution)/shard_map/all_gather | solution.py:113
  481.6 6.0 %copy.30 = f32[52,8,16,256]{3,2,1,0:T(8,128)S(1)} copy(f32[52,8,16,256]{3,1,2,0:T(8,128)} %bitcast.32) | data formatting | bytes 13631488
  487.6 0.0 copy-start.2
  487.7 1.2 bitcast_reduce_fusion
  488.9 1.0 copy.28
  489.9 12.6 %all-to-all-start.1 = ((f32[32,8,411]{2,1,0:T(8,128)}), f32[32,8,411]{2,1,0:T(8,128)S(1)}, u32[]{:S(2)}, u32[]{:S(2)}) async-start(f32[32,8,411]{2,1,0:T(8,128)} %bitcast.5), calls=%async_computation.1 | async-start | bytes 1048576 | tf_op jit(solution)/shard_map/all_to_all | solution.py:114
  502.5 3.4 collective-permute-start.2
  505.9 2.5 collective-permute-start
  508.4 0.2 dynamic-slice_reduce_fusion.2
  508.6 4.8 collective-permute-done
  513.5 0.1 fusion.41
  513.6 1.7 collective-permute-start.4
  515.2 21.3 %all-to-all-done.1 = f32[32,8,411]{2,1,0:T(8,128)S(1)} async-done(((f32[32,8,411]{2,1,0:T(8,128)}), f32[32,8,411]{2,1,0:T(8,128)S(1)}, u32[]{:S(2)}, u32[]{:S(2)}) %all-to-all-start.1) | async-done | bytes 420896 | tf_op jit(solution)/shard_map/all_to_all | solution.py:114
  536.5 0.6 gather_fusion
  537.1 0.1 select_multiply_fusion
  537.2 3.4 collective-permute-start.3
  540.6 2.5 collective-permute-start.1
  543.1 0.1 pad_maximum_fusion.25
  543.2 0.2 collective-permute-done.3
  543.4 5.5 collective-permute-done.1
  548.9 0.0 collective-permute-start.5
  548.9 0.5 collective-permute-start.7
  549.4 0.1 slice_multiply_fusion.3
  549.5 0.8 collective-permute-done.5
  550.3 2.9 collective-permute-done.7
  553.3 0.2 fusion.23
  553.5 1.9 collective-permute-start.9
  555.5 3.9 collective-permute-start.8
  559.4 0.3 collective-permute-done.9
  559.7 4.0 collective-permute-done.8
  563.7 0.0 collective-permute-start.10
  563.8 0.5 collective-permute-start.11
  564.3 0.9 collective-permute-done.10
  565.2 2.9 collective-permute-done.11
  568.1 0.9 fusion.11
  (36 shorter events, 0.3 us)
Async XLA Ops:
  6.5 116.4 %copy-start = (bf16[2048,384]{1,0:T(8,128)(2,1)S(1)}, bf16[2048,384]{1,0:T(8,128)(2,1)}, u32[]{:S(2)}) copy-start(bf16[2048,384]{1,0:T(8,128)(2,1)} %param.17) | copy-start | bytes 4718596
  6.5 67.7 %copy-start.1 = (bf16[411,128]{1,0:T(8,128)(2,1)S(1)}, bf16[411,128]{1,0:T(8,128)(2,1)}, u32[]{:S(2)}) copy-start(bf16[411,128]{1,0:T(8,128)(2,1)} %param.15) | copy-start | bytes 315652
  6.5 67.7 %copy-start.6 = (f32[128]{0:T(128)S(1)}, f32[128]{0:T(128)}, u32[]{:S(2)}) copy-start(f32[128]{0:T(128)} %param.16) | copy-start | bytes 1540
  6.5 69.0 %copy-start.3 = (s32[256]{0:T(256)S(1)}, s32[256]{0:T(256)}, u32[]{:S(2)}) copy-start(s32[256]{0:T(256)} %param.14) | copy-start | bytes 3076
  6.5 116.4 %copy-start.5 = (f32[384]{0:T(512)S(1)}, f32[384]{0:T(512)}, u32[]{:S(2)}) copy-start(f32[384]{0:T(512)} %param.18) | copy-start | bytes 4612
  6.5 116.4 %copy-start.4 = (bf16[256,384]{1,0:T(8,128)(2,1)S(1)}, bf16[256,384]{1,0:T(8,128)(2,1)}, u32[]{:S(2)}) copy-start(bf16[256,384]{1,0:T(8,128)(2,1)} %param.13) | copy-start | bytes 589828
  6.6 116.4 %all-gather.6.cloned.1.call-start = ((), (), s32[]{:S(2)}) async-start(), calls=%async_computation.2 | async-start | bytes 1114112 | tf_op jit(solution)/shard_map/all_gather | solution.py:84
  75.1 117.4 %all-gather.8.cloned.1.call-start = ((), (), s32[]{:S(2)}) async-start(), calls=%async_computation.3 | async-start | bytes 3342336 | tf_op jit(solution)/shard_map/all_gather | solution.py:92
  125.6 142.8 %all-gather.10.cloned.1.call-start = ((), (), s32[]{:S(2)}) async-start(), calls=%async_computation.4 | async-start | bytes 4866048 | tf_op jit(solution)/shard_map/all_gather | solution.py:96
  126.3 268.1 %all-reduce.2.cloned.1.call-start = ((), (), s32[]{:S(2)}) async-start(), calls=%async_computation.5 | async-start | bytes 4194304 | tf_op jit(solution)/shard_map/psum | solution.py:101
  275.5 206.1 %all-gather.12.cloned.1.call-start = ((), (), s32[]{:S(2)}) async-start(), calls=%async_computation.6 | async-start | bytes 7241728 | tf_op jit(solution)/shard_map/all_gather | solution.py:113
  487.6 14.9 %copy-start.2 = (f32[4,32]{1,0:T(4,128)S(1)}, f32[4,32]{1,0:T(4,128)}, u32[]{:S(2)}) copy-start(f32[4,32]{1,0:T(4,128)} %param.11) | copy-start | bytes 1540
  489.9 46.6 %all-to-all-start.1 = ((f32[32,8,411]{2,1,0:T(8,128)}), f32[32,8,411]{2,1,0:T(8,128)S(1)}, u32[]{:S(2)}, u32[]{:S(2)}) async-start(f32[32,8,411]{2,1,0:T(8,128)} %bitcast.5), calls=%async_computation.1 | async-start | bytes 1048576 | tf_op jit(solution)/shard_map/all_to_all | solution.py:114
  502.5 6.1 %collective-permute-start.2 = (f32[1,32]{1,0:T(1,128)S(1)}, f32[1,32]{1,0:T(1,128)S(1)}, u32[]{:S(2)}, u32[]{:S(2)}) collective-permute-start(f32[1,32]{1,0:T(1,128)S(1)} %get-tuple-element.23), channel_id=1, source_target_pairs={{0,1},{1,2},{2,3},{3,4},{4,5},{5,6},{6,7},{7,8},{8,9},{9,10},{10,1... | collective-permute-start | bytes 392 | tf_op jit(solution)/shard_map/ppermute | solution.py:14
  505.9 7.6 %collective-permute-start = (f32[1,32]{1,0:T(1,128)S(1)}, f32[1,32]{1,0:T(1,128)S(1)}, u32[]{:S(2)}, u32[]{:S(2)}) collective-permute-start(f32[1,32]{1,0:T(1,128)S(1)} %get-tuple-element.24), channel_id=1, source_target_pairs={{1,0},{2,1},{3,2},{4,3},{5,4},{6,5},{7,6},{8,7},{9,8},{10,9},{11,1... | collective-permute-start | bytes 392 | tf_op jit(solution)/shard_map/ppermute | solution.py:15
  513.6 29.5 %collective-permute-start.4 = (f32[6,1]{1,0:T(8,128)S(1)}, f32[6,1]{1,0:T(8,128)S(1)}, u32[]{:S(2)}, u32[]{:S(2)}) collective-permute-start(f32[6,1]{1,0:T(8,128)S(1)} %get-tuple-element.13), channel_id=1, source_target_pairs={{16,0},{32,16},{48,32},{64,48},{80,64},{96,80},{112,96},{128,112},... | collective-permute-start | bytes 80 | tf_op jit(solution)/shard_map/ppermute | solution.py:15
  515.2 27.8 %collective-permute-start.6 = (f32[6,1]{1,0:T(8,128)S(1)}, f32[6,1]{1,0:T(8,128)S(1)}, u32[]{:S(2)}, u32[]{:S(2)}) collective-permute-start(f32[6,1]{1,0:T(8,128)S(1)} %get-tuple-element.14), channel_id=1, source_target_pairs={{0,16},{16,32},{32,48},{48,64},{64,80},{80,96},{96,112},{112,128},... | collective-permute-start | bytes 80 | tf_op jit(solution)/shard_map/ppermute | solution.py:14
  537.2 6.2 %collective-permute-start.3 = (f32[1,32,411]{2,1,0:T(8,128)S(1)}, f32[1,32,411]{2,1,0:T(8,128)S(1)}, u32[]{:S(2)}, u32[]{:S(2)}) collective-permute-start(f32[1,32,411]{2,1,0:T(8,128)S(1)} %mul.151), channel_id=1, source_target_pairs={{0,1},{1,2},{2,3},{3,4},{4,5},{5,6},{6,7},{7,8},{8,9},{9,10},{10,1... | collective-permute-start | bytes 157832 | tf_op jit(solution)/shard_map/ppermute | solution.py:14
  540.6 8.3 %collective-permute-start.1 = (f32[1,32,411]{2,1,0:T(8,128)S(1)}, f32[1,32,411]{2,1,0:T(8,128)S(1)}, u32[]{:S(2)}, u32[]{:S(2)}) collective-permute-start(f32[1,32,411]{2,1,0:T(8,128)S(1)} %mul.151), channel_id=1, source_target_pairs={{1,0},{2,1},{3,2},{4,3},{5,4},{6,5},{7,6},{8,7},{9,8},{10,9},{11,1... | collective-permute-start | bytes 157832 | tf_op jit(solution)/shard_map/ppermute | solution.py:15
  548.9 1.4 collective-permute-start.5
  548.9 4.3 collective-permute-start.7
  553.5 6.2 %collective-permute-start.9 = (f32[1,32,411]{2,1,0:T(8,128)S(1)}, f32[1,32,411]{2,1,0:T(8,128)S(1)}, u32[]{:S(2)}, u32[]{:S(2)}) collective-permute-start(f32[1,32,411]{2,1,0:T(8,128)S(1)} %get-tuple-element.11), channel_id=1, source_target_pairs={{0,1},{1,2},{2,3},{3,4},{4,5},{5,6},{6,7},{7,8},{8,9},{9,10},{10,1... | collective-permute-start | bytes 157832 | tf_op jit(solution)/shard_map/ppermute | solution.py:14
  555.5 8.3 %collective-permute-start.8 = (f32[1,32,411]{2,1,0:T(8,128)S(1)}, f32[1,32,411]{2,1,0:T(8,128)S(1)}, u32[]{:S(2)}, u32[]{:S(2)}) collective-permute-start(f32[1,32,411]{2,1,0:T(8,128)S(1)} %get-tuple-element.12), channel_id=1, source_target_pairs={{1,0},{2,1},{3,2},{4,3},{5,4},{6,5},{7,6},{8,7},{9,8},{10,9},{11,1... | collective-permute-start | bytes 157832 | tf_op jit(solution)/shard_map/ppermute | solution.py:15
  563.7 1.4 collective-permute-start.10
  563.8 4.3 collective-permute-start.11
Sparse Core Ops, SparseCore 0:
  75.2 47.6 all-gather.5
  125.9 66.5 all-gather.7
  194.7 73.6 all-gather.9
  275.7 118.6 all-reduce.1
  397.2 84.3 all-gather.11
